TPU v7x, 128 devices: a whole 4x4x4 slice. The times are simulated.
128 devices in a mesh: vox: 8 (over y, core), fas: 16 (over z, x).
Axes of the slice: x: 4, y: 4, z: 4, core: 2. Of those that a mesh axis runs over, the one named last changes fastest.
Arguments:
- signal: float32 [128, 6144], P('vox', 'fas'), may hold values from -6 to 6
- initial_weights: float32 [524288], P('fas'), may hold values from 0.1 to 2
- coefficients: bfloat16 [32768, 4096], P(('vox', 'fas')), may hold values from 0 to 0.0234375
- block_rows: int32 [32768], P(('vox', 'fas')), may hold values from 0 to 127, as said below
- block_cols: int32 [32768], P(('vox', 'fas')), may hold values from 0 to 8191, as said below
- block_atoms: int32 [32768, 64], P(('vox', 'fas')), may hold values from 0 to 359
- block_count: int32 [128], P(('vox', 'fas')), may hold values from 64 to 256, as said below
- dictionary: bfloat16 [360, 96], replicated, may hold values from -6 to 6
Outputs:
- weights: float32 [524288], P('fas')
- residual: float32 [128, 6144], P('vox', 'fas')
Inputs may be any that keep to these rules, and one draw needn't show every extreme that they name: Block slots are stored device by device: the device with vox index i and fas index f holds slots (i * 16 + f) * 256 to (i * 16 + f + 1) * 256 - 1, and every block_rows value there lies in i * 16 to (i + 1) * 16 - 1. For the slots of the device with fas index f, every block_cols value lies in f * 512 to (f + 1) * 512 - 1. `block_count`: entry i * 16 + f is the number of live slots of the device with vox index i and fas index f, its first slots; some device has all 256 live.
All inputs are finite; a program needn't handle non-finite values.
Results may differ from a plain program's by a relative error of at most 0.0003.
Values sent between devices are 32-bit elements; how exact they have to be, the bound alone decides.
A program may use at most 128 MiB of HBM per device.

v0:
```python
import jax
import jax.numpy as jnp
from jax import lax
from jax.sharding import PartitionSpec as P

BV = 64
BF = 64
DIRS = 96
ITERS = 5


def local(
    signal,
    initial_weights,
    coefficients,
    block_rows,
    block_cols,
    block_atoms,
    block_count,
    dictionary,
):
    vox_rows = signal.shape[0]
    fas_rows = initial_weights.shape[0] // BF
    slot_total = coefficients.shape[0]
    row_width = BV * DIRS
    fas_place = lax.axis_index("fas")
    rows_local = block_rows - lax.axis_index("vox") * vox_rows
    cols_local = block_cols - fas_place * fas_rows
    live_count = block_count[0]
    atom_table = dictionary[block_atoms]
    coef_view = coefficients.reshape(slot_total, BV, BF)
    group_size = min(256, slot_total)
    group_turns = (live_count + group_size - 1) // group_size
    vox_range = jnp.arange(vox_rows, dtype=jnp.int32)
    fas_range = jnp.arange(fas_rows, dtype=jnp.int32)

    def group_pieces(first_slot):
        live_mask = (first_slot + jnp.arange(group_size, dtype=jnp.int32) < live_count).astype(
            jnp.float32
        )
        return (coef_view, atom_table, rows_local, cols_local, live_mask)

    def forward_partial(values):
        table = values.reshape(fas_rows, BF)

        def forward_accumulate(turn, running):
            coef_blk, atom_blk, rows_blk, cols_blk, live_mask = group_pieces(turn * group_size)
            scaled = coef_blk.astype(jnp.float32) * table[cols_blk][:, None, :]
            image_blk = jnp.einsum(
                "kvj,kjd->kvd",
                scaled,
                atom_blk.astype(jnp.float32),
                precision=lax.Precision.HIGHEST,
                preferred_element_type=jnp.float32,
            )
            selector = (rows_blk[:, None] == vox_range[None, :]).astype(jnp.float32) * live_mask[
                :, None
            ]
            added = jnp.dot(
                selector.T,
                image_blk.reshape(group_size, row_width),
                precision=lax.Precision.HIGHEST,
                preferred_element_type=jnp.float32,
            )
            return running + added

        start = jnp.zeros((vox_rows, row_width), jnp.float32)
        return lax.fori_loop(0, group_turns, forward_accumulate, start)

    def backward_partial(rows_view):

        def backward_accumulate(turn, running):
            coef_blk, atom_blk, rows_blk, cols_blk, live_mask = group_pieces(turn * group_size)
            gathered = rows_view[rows_blk]
            inner = jnp.einsum(
                "kvj,kvd->kjd",
                coef_blk.astype(jnp.float32),
                gathered,
                precision=lax.Precision.HIGHEST,
                preferred_element_type=jnp.float32,
            )
            contrib = jnp.sum(atom_blk.astype(jnp.float32) * inner, axis=-1)
            selector = (cols_blk[:, None] == fas_range[None, :]).astype(jnp.float32) * live_mask[
                :, None
            ]
            added = jnp.dot(
                selector.T,
                contrib,
                precision=lax.Precision.HIGHEST,
                preferred_element_type=jnp.float32,
            )
            return running + added

        start = jnp.zeros((fas_rows, BF), jnp.float32)
        running = lax.fori_loop(0, group_turns, backward_accumulate, start)
        return running.reshape(-1)

    def collect(partial_value):
        return lax.psum_scatter(partial_value, "fas", scatter_dimension=1, tiled=True)

    weights = initial_weights
    residual = collect(forward_partial(weights)) - signal
    for sweep in range(ITERS):
        whole_rows = lax.all_gather(residual, "fas", axis=1, tiled=True)
        gradient = lax.psum(backward_partial(whole_rows.reshape(vox_rows, BV, DIRS)), "vox")
        projected = jnp.where((weights > 0) | (gradient < 0), gradient, 0.0)
        image_pred = collect(forward_partial(projected))
        image_local = jnp.sum(image_pred * image_pred)
        grad_sq = lax.psum(jnp.sum(projected * projected), "fas")
        image_sq = lax.psum(image_local, ("vox", "fas"))
        step_size = grad_sq / (image_sq + 1e-06)
        weights = jnp.maximum(weights - step_size * projected, 0.0)
        residual = collect(forward_partial(weights)) - signal
    return (weights, residual)


def solution(mesh):
    placed = (
        P("vox", "fas"),
        P("fas"),
        P(("vox", "fas"), None),
        P(("vox", "fas")),
        P(("vox", "fas")),
        P(("vox", "fas"), None),
        P(("vox", "fas")),
        P(),
    )
    return jax.shard_map(
        local, mesh=mesh, in_specs=placed, out_specs=(P("fas"), P("vox", "fas")), check_vma=False
    )
```

profile of v0, /device:TPU:0, one launch (start us, length us, event | category | flops | bytes accessed | tf_op | source)
XLA Modules:
  0.0 2227.8 jit_solution(15539309578874618926)
XLA Ops:
  18.6 57.4 %gather_fusion = bf16[16384,96]{1,0:T(8,128)(2,1)} fusion(bf16[360,96]{1,0:T(8,128)(2,1)S(1)} %copy.28, s32[16384]{0:T(1024)S(1)} %broadcast_clamp_fusion), kind=kCustom, calls=%fused_computation | custom fusion | bytes 6356992 | tf_op jit(solution)/shard_map/gather | solution.py:30
  105.5 74.3 %reduce-scatter.12.cloned.1.call-done = f32[16,384]{1,0:T(8,128)} async-done(((f32[16,6144]{1,0:T(8,128)}), f32[16,384]{1,0:T(8,128)}) %reduce-scatter.12.cloned.1.call-update) | async-done | bytes 24592 | tf_op jit(solution)/shard_map/reduce_scatter | solution.py:99
  224.2 58.0 %all-reduce.6.cloned.1.call-done = f32[32768]{0:T(1024)} async-done(((f32[32768]{0:T(1024)}), f32[32768]{0:T(1024)}) %all-reduce.6.cloned.1.call-update) | async-done | bytes 131088 | tf_op jit(solution)/shard_map/psum | solution.py:105
  284.7 28.3 %while.210 = (s32[]{:T(128)}, f32[16,6144]{1,0:T(8,128)S(1)}, s32[]{:T(128)}, s32[256]{0:T(256)S(1)}, s32[]{:T(128)}, /*index=5*/bf16[256,64,64]{2,1,0:T(8,128)(...) while((s32[]{:T(128)}, f32[16,6144]{1,0:T(8,128)S(1)}, ...), condition=%wide.region_10.11_spmd.clone, body=%wide.region_9.10_spmd.clone.sunk | while | flops 1512153856 | bytes 31263864 | solution.py:68
  313.8 70.8 %reduce-scatter.14.cloned.1.call-done = f32[16,384]{1,0:T(8,128)} async-done(((f32[16,6144]{1,0:T(8,128)}), f32[16,384]{1,0:T(8,128)}) %reduce-scatter.14.cloned.1.call-update) | async-done | bytes 24592 | tf_op jit(solution)/shard_map/reduce_scatter | solution.py:99
  386.1 38.8 %psum.106 = f32[]{:T(128)} all-reduce(f32[]{:T(128)} %get-tuple-element.2460), channel_id=1, replica_groups=mesh['vox'=8,'fas'=16] {'fas'}, use_global_device_ids=true, to_apply=%region_8.9 | all-reduce | flops 1 | bytes 8 | tf_op jit(solution)/shard_map/psum | solution.py:109
  424.8 62.7 %psum.107 = f32[]{:T(128)} all-reduce(f32[]{:T(128)} %multiply_reduce_fusion.9), channel_id=1, replica_groups=mesh['vox'=8,'fas'=16] {'vox','fas'}, use_global_device_ids=true, to_apply=%region_13.14 | all-reduce | flops 1 | bytes 8 | tf_op jit(solution)/shard_map/psum | solution.py:110
  518.7 69.0 %reduce-scatter.16.cloned.1.call-done = f32[16,384]{1,0:T(8,128)} async-done(((f32[16,6144]{1,0:T(8,128)}), f32[16,384]{1,0:T(8,128)}) %reduce-scatter.16.cloned.1.call-update) | async-done | bytes 24592 | tf_op jit(solution)/shard_map/reduce_scatter | solution.py:99
  632.2 58.0 %all-reduce.8.cloned.1.call-done = f32[32768]{0:T(1024)} async-done(((f32[32768]{0:T(1024)}), f32[32768]{0:T(1024)}) %all-reduce.8.cloned.1.call-update) | async-done | bytes 131088 | tf_op jit(solution)/shard_map/psum | solution.py:105
  692.7 28.2 %while.213 = (s32[]{:T(128)}, f32[16,6144]{1,0:T(8,128)S(1)}, s32[]{:T(128)}, s32[256]{0:T(256)S(1)}, s32[]{:T(128)}, /*index=5*/bf16[256,64,64]{2,1,0:T(8,128)(...) while((s32[]{:T(128)}, f32[16,6144]{1,0:T(8,128)S(1)}, ...), condition=%wide.region_24.25_spmd.clone, body=%wide.region_23.24_spmd.clone.sunk | while | flops 1512153856 | bytes 31263864 | solution.py:68
  721.7 70.8 %reduce-scatter.18.cloned.1.call-done = f32[16,384]{1,0:T(8,128)} async-done(((f32[16,6144]{1,0:T(8,128)}), f32[16,384]{1,0:T(8,128)}) %reduce-scatter.18.cloned.1.call-update) | async-done | bytes 24592 | tf_op jit(solution)/shard_map/reduce_scatter | solution.py:99
  793.8 38.8 %psum.109 = f32[]{:T(128)} all-reduce(f32[]{:T(128)} %get-tuple-element.2458), channel_id=1, replica_groups=mesh['vox'=8,'fas'=16] {'fas'}, use_global_device_ids=true, to_apply=%region_22.23 | all-reduce | flops 1 | bytes 8 | tf_op jit(solution)/shard_map/psum | solution.py:109
  832.6 62.8 %psum.110 = f32[]{:T(128)} all-reduce(f32[]{:T(128)} %multiply_reduce_fusion.8), channel_id=1, replica_groups=mesh['vox'=8,'fas'=16] {'vox','fas'}, use_global_device_ids=true, to_apply=%region_27.28 | all-reduce | flops 1 | bytes 8 | tf_op jit(solution)/shard_map/psum | solution.py:110
  897.6 28.4 %while.214 = (s32[]{:T(128)}, f32[16,6144]{1,0:T(8,128)S(1)}, s32[]{:T(128)}, s32[256]{0:T(256)S(1)}, s32[]{:T(128)}, /*index=5*/bf16[256,64,64]{2,1,0:T(8,128)(...) while((s32[]{:T(128)}, f32[16,6144]{1,0:T(8,128)S(1)}, ...), condition=%wide.region_29.30_spmd.clone, body=%wide.region_28.29_spmd.clone.sunk | while | flops 1512153856 | bytes 31263864 | solution.py:68
  926.8 69.0 %reduce-scatter.20.cloned.1.call-done = f32[16,384]{1,0:T(8,128)} async-done(((f32[16,6144]{1,0:T(8,128)}), f32[16,384]{1,0:T(8,128)}) %reduce-scatter.20.cloned.1.call-update) | async-done | bytes 24592 | tf_op jit(solution)/shard_map/reduce_scatter | solution.py:99
  1040.3 58.0 %all-reduce.10.cloned.1.call-done = f32[32768]{0:T(1024)} async-done(((f32[32768]{0:T(1024)}), f32[32768]{0:T(1024)}) %all-reduce.10.cloned.1.call-update) | async-done | bytes 131088 | tf_op jit(solution)/shard_map/psum | solution.py:105
  1129.6 70.8 %reduce-scatter.22.cloned.1.call-done = f32[16,384]{1,0:T(8,128)} async-done(((f32[16,6144]{1,0:T(8,128)}), f32[16,384]{1,0:T(8,128)}) %reduce-scatter.22.cloned.1.call-update) | async-done | bytes 24592 | tf_op jit(solution)/shard_map/reduce_scatter | solution.py:99
  1201.9 38.8 %psum.112 = f32[]{:T(128)} all-reduce(f32[]{:T(128)} %get-tuple-element.2456), channel_id=1, replica_groups=mesh['vox'=8,'fas'=16] {'fas'}, use_global_device_ids=true, to_apply=%region_36.37 | all-reduce | flops 1 | bytes 8 | tf_op jit(solution)/shard_map/psum | solution.py:109
  1240.6 62.7 %psum.113 = f32[]{:T(128)} all-reduce(f32[]{:T(128)} %multiply_reduce_fusion.7), channel_id=1, replica_groups=mesh['vox'=8,'fas'=16] {'vox','fas'}, use_global_device_ids=true, to_apply=%region_41.42 | all-reduce | flops 1 | bytes 8 | tf_op jit(solution)/shard_map/psum | solution.py:110
  1305.6 28.3 %while.217 = (s32[]{:T(128)}, f32[16,6144]{1,0:T(8,128)S(1)}, s32[]{:T(128)}, s32[256]{0:T(256)S(1)}, s32[]{:T(128)}, /*index=5*/bf16[256,64,64]{2,1,0:T(8,128)(...) while((s32[]{:T(128)}, f32[16,6144]{1,0:T(8,128)S(1)}, ...), condition=%wide.region_43.44_spmd.clone, body=%wide.region_42.43_spmd.clone.sunk | while | flops 1512153856 | bytes 31263864 | solution.py:68
  1334.7 69.1 %reduce-scatter.24.cloned.1.call-done = f32[16,384]{1,0:T(8,128)} async-done(((f32[16,6144]{1,0:T(8,128)}), f32[16,384]{1,0:T(8,128)}) %reduce-scatter.24.cloned.1.call-update) | async-done | bytes 24592 | tf_op jit(solution)/shard_map/reduce_scatter | solution.py:99
  1448.3 57.9 %all-reduce.12.cloned.1.call-done = f32[32768]{0:T(1024)} async-done(((f32[32768]{0:T(1024)}), f32[32768]{0:T(1024)}) %all-reduce.12.cloned.1.call-update) | async-done | bytes 131088 | tf_op jit(solution)/shard_map/psum | solution.py:105
  1537.6 70.8 %reduce-scatter.26.cloned.1.call-done = f32[16,384]{1,0:T(8,128)} async-done(((f32[16,6144]{1,0:T(8,128)}), f32[16,384]{1,0:T(8,128)}) %reduce-scatter.26.cloned.1.call-update) | async-done | bytes 24592 | tf_op jit(solution)/shard_map/reduce_scatter | solution.py:99
  1609.8 38.8 %psum.115 = f32[]{:T(128)} all-reduce(f32[]{:T(128)} %get-tuple-element.2454), channel_id=1, replica_groups=mesh['vox'=8,'fas'=16] {'fas'}, use_global_device_ids=true, to_apply=%region_50.51 | all-reduce | flops 1 | bytes 8 | tf_op jit(solution)/shard_map/psum | solution.py:109
  1648.6 62.8 %psum.116 = f32[]{:T(128)} all-reduce(f32[]{:T(128)} %multiply_reduce_fusion.6), channel_id=1, replica_groups=mesh['vox'=8,'fas'=16] {'vox','fas'}, use_global_device_ids=true, to_apply=%region_55.56 | all-reduce | flops 1 | bytes 8 | tf_op jit(solution)/shard_map/psum | solution.py:110
  1713.6 28.3 %while.220 = (s32[]{:T(128)}, f32[16,6144]{1,0:T(8,128)S(1)}, s32[]{:T(128)}, s32[256]{0:T(256)S(1)}, s32[]{:T(128)}, /*index=5*/bf16[256,64,64]{2,1,0:T(8,128)(...) while((s32[]{:T(128)}, f32[16,6144]{1,0:T(8,128)S(1)}, ...), condition=%wide.region_57.58_spmd.clone, body=%wide.region_56.57_spmd.clone.sunk | while | flops 1512153856 | bytes 31263864 | solution.py:68
  1742.7 69.0 %reduce-scatter.28.cloned.1.call-done = f32[16,384]{1,0:T(8,128)} async-done(((f32[16,6144]{1,0:T(8,128)}), f32[16,384]{1,0:T(8,128)}) %reduce-scatter.28.cloned.1.call-update) | async-done | bytes 24592 | tf_op jit(solution)/shard_map/reduce_scatter | solution.py:99
  1856.2 58.0 %all-reduce.14.cloned.1.call-done = f32[32768]{0:T(1024)} async-done(((f32[32768]{0:T(1024)}), f32[32768]{0:T(1024)}) %all-reduce.14.cloned.1.call-update) | async-done | bytes 131088 | tf_op jit(solution)/shard_map/psum | solution.py:105
  1945.5 70.8 %reduce-scatter.30.cloned.1.call-done = f32[16,384]{1,0:T(8,128)} async-done(((f32[16,6144]{1,0:T(8,128)}), f32[16,384]{1,0:T(8,128)}) %reduce-scatter.30.cloned.1.call-update) | async-done | bytes 24592 | tf_op jit(solution)/shard_map/reduce_scatter | solution.py:99
  2017.8 38.8 %psum.118 = f32[]{:T(128)} all-reduce(f32[]{:T(128)} %get-tuple-element.2452), channel_id=1, replica_groups=mesh['vox'=8,'fas'=16] {'fas'}, use_global_device_ids=true, to_apply=%region_64.65 | all-reduce | flops 1 | bytes 8 | tf_op jit(solution)/shard_map/psum | solution.py:109
  2056.5 62.7 %psum.119 = f32[]{:T(128)} all-reduce(f32[]{:T(128)} %multiply_reduce_fusion.5), channel_id=1, replica_groups=mesh['vox'=8,'fas'=16] {'vox','fas'}, use_global_device_ids=true, to_apply=%region_69.70 | all-reduce | flops 1 | bytes 8 | tf_op jit(solution)/shard_map/psum | solution.py:110
  2150.5 69.0 %reduce-scatter.32.cloned.1.call-done = f32[16,384]{1,0:T(8,128)} async-done(((f32[16,6144]{1,0:T(8,128)}), f32[16,384]{1,0:T(8,128)}) %reduce-scatter.32.cloned.1.call-update) | async-done | bytes 24592 | tf_op jit(solution)/shard_map/reduce_scatter | solution.py:99
  (233 shorter events, 748.5 us)
Async XLA Ops:
  7.2 10.8 copy-start.15
  7.2 11.1 copy-start.14
  7.2 11.2 copy-start.16
  7.2 11.2 copy-start.11
  7.2 172.5 %reduce-scatter.12.cloned.1.call-start = ((), (), s32[]{:S(2)}) async-start(), calls=%async_computation.11 | async-start | bytes 417792 | tf_op jit(solution)/shard_map/reduce_scatter | solution.py:99
  18.5 58.1 %copy-start.17 = (s32[256]{0:T(256)S(1)}, s32[256]{0:T(256)}, u32[]{:S(2)}) copy-start(s32[256]{0:T(256)} %param.43) | copy-start | bytes 3076
  76.7 103.0 %copy-start.12 = (f32[16,384]{1,0:T(8,128)S(1)}, f32[16,384]{1,0:T(8,128)}, u32[]{:S(2)}) copy-start(f32[16,384]{1,0:T(8,128)} %param.40) | copy-start | bytes 73732
  104.6 0.7 copy-start.1
  105.4 176.9 %all-reduce.6.cloned.1.call-start = ((), (), s32[]{:S(2)}) async-start(), calls=%async_computation.12 | async-start | bytes 262144 | tf_op jit(solution)/shard_map/psum | solution.py:105
  224.2 160.4 %reduce-scatter.14.cloned.1.call-start = ((), (), s32[]{:S(2)}) async-start(), calls=%async_computation.13 | async-start | bytes 417792 | tf_op jit(solution)/shard_map/reduce_scatter | solution.py:99
  313.0 0.7 copy-start.2
  313.8 274.0 %reduce-scatter.16.cloned.1.call-start = ((), (), s32[]{:S(2)}) async-start(), calls=%async_computation.14 | async-start | bytes 417792 | tf_op jit(solution)/shard_map/reduce_scatter | solution.py:99
  517.9 0.7 copy-start.3
  518.7 171.6 %all-reduce.8.cloned.1.call-start = ((), (), s32[]{:S(2)}) async-start(), calls=%async_computation.15 | async-start | bytes 262144 | tf_op jit(solution)/shard_map/psum | solution.py:105
  632.2 160.2 %reduce-scatter.18.cloned.1.call-start = ((), (), s32[]{:S(2)}) async-start(), calls=%async_computation.16 | async-start | bytes 417792 | tf_op jit(solution)/shard_map/reduce_scatter | solution.py:99
  721.6 274.2 %reduce-scatter.20.cloned.1.call-start = ((), (), s32[]{:S(2)}) async-start(), calls=%async_computation.17 | async-start | bytes 417792 | tf_op jit(solution)/shard_map/reduce_scatter | solution.py:99
  926.8 171.5 %all-reduce.10.cloned.1.call-start = ((), (), s32[]{:S(2)}) async-start(), calls=%async_computation.18 | async-start | bytes 262144 | tf_op jit(solution)/shard_map/psum | solution.py:105
  1040.2 160.2 %reduce-scatter.22.cloned.1.call-start = ((), (), s32[]{:S(2)}) async-start(), calls=%async_computation.19 | async-start | bytes 417792 | tf_op jit(solution)/shard_map/reduce_scatter | solution.py:99
  1128.8 0.7 copy-start.6
  1129.6 274.2 %reduce-scatter.24.cloned.1.call-start = ((), (), s32[]{:S(2)}) async-start(), calls=%async_computation.20 | async-start | bytes 417792 | tf_op jit(solution)/shard_map/reduce_scatter | solution.py:99
  1333.9 0.7 copy-start.7
  1334.7 171.5 %all-reduce.12.cloned.1.call-start = ((), (), s32[]{:S(2)}) async-start(), calls=%async_computation.21 | async-start | bytes 262144 | tf_op jit(solution)/shard_map/psum | solution.py:105
  1448.2 160.2 %reduce-scatter.26.cloned.1.call-start = ((), (), s32[]{:S(2)}) async-start(), calls=%async_computation.22 | async-start | bytes 417792 | tf_op jit(solution)/shard_map/reduce_scatter | solution.py:99
  1536.8 0.7 copy-start.8
  1537.5 274.2 %reduce-scatter.28.cloned.1.call-start = ((), (), s32[]{:S(2)}) async-start(), calls=%async_computation.23 | async-start | bytes 417792 | tf_op jit(solution)/shard_map/reduce_scatter | solution.py:99
  1741.9 0.7 copy-start.9
  1742.7 171.5 %all-reduce.14.cloned.1.call-start = ((), (), s32[]{:S(2)}) async-start(), calls=%async_computation.24 | async-start | bytes 262144 | tf_op jit(solution)/shard_map/psum | solution.py:105
  1856.1 160.2 %reduce-scatter.30.cloned.1.call-start = ((), (), s32[]{:S(2)}) async-start(), calls=%async_computation.25 | async-start | bytes 417792 | tf_op jit(solution)/shard_map/reduce_scatter | solution.py:99
  1944.7 0.7 copy-start.10
  1945.5 274.0 %reduce-scatter.32.cloned.1.call-start = ((), (), s32[]{:S(2)}) async-start(), calls=%async_computation.26 | async-start | bytes 417792 | tf_op jit(solution)/shard_map/reduce_scatter | solution.py:99
  2120.6 0.9 copy-start.13
  2149.7 0.7 copy-start
  (2 other events, 1.5 us)
Sparse Core Ops, SparseCore 0:
  105.5 74.1 reduce-scatter.11
  224.3 57.9 all-reduce.5
  313.9 70.6 reduce-scatter.13
  518.8 68.9 reduce-scatter.15
  632.3 57.8 all-reduce.7
  721.7 70.6 reduce-scatter.17
  926.9 68.9 reduce-scatter.19
  1040.4 57.8 all-reduce.9
  1129.7 70.6 reduce-scatter.21
  1334.8 68.9 reduce-scatter.23
  1448.3 57.8 all-reduce.11
  1537.7 70.6 reduce-scatter.25
  1742.8 68.9 reduce-scatter.27
  1856.3 57.8 all-reduce.13
  1945.6 70.6 reduce-scatter.29
  2150.6 68.8 reduce-scatter.31
where the time goes:
time: 2240 us; the launch traced here: 2230 us
  waiting for transfers between devices  1060 us (47%)
  blocking collectives  625 us (28%)
  matrix products  275 us (12%)
  local copies, waits for them, and re-layouts  207 us (9%)
  other arithmetic  30.5 us (1%)
  between operations  22.5 us (1%)
    reduce_scatter x11, waiting for transfers between devices, collect(): lax.psum_scatter(partial_value, 'fas', scatter_dimension=1, tiled=True)  773 us
    psum x5, blocking collectives, local(): image_sq = lax.psum(image_local, ('vox', 'fas'))  314 us
    psum x5, waiting for transfers between devices, local(): lax.psum(backward_partial(whole_rows.reshape(vox_rows, BV, DIRS)), 'vox')  290 us
    psum x5, blocking collectives, local(): grad_sq = lax.psum(jnp.sum(projected * projected), 'fas')  194 us
    dot_general x11, matrix products, forward_accumulate(): jnp.einsum('kvj,kjd->kvd', scaled, atom_blk.astype(jnp.float32), precisio...  124 us
    all_gather x5, blocking collectives, local(): whole_rows = lax.all_gather(residual, 'fas', axis=1, tiled=True)  118 us
    dot_general x11, local copies, waits for them, and re-layouts, forward_accumulate(): jnp.einsum('kvj,kjd->kvd', scaled, atom_blk.astype(jnp.float32), precisio...  94.4 us
    dot_general x11, matrix products, forward_accumulate(): jnp.dot(selector.T, image_blk.reshape(group_size, row_width), precision=l...  81.8 us
  transfers between devices with their start and end apart: 16, of which 16 were waited for; matrix products, arithmetic and copies ran while one was open for 0% of the time, Pallas kernels for 0%

commit v1 on v0

--- a/solution.py
+++ b/solution.py
@@ -101,7 +101,18 @@
     weights = initial_weights
     residual = collect(forward_partial(weights)) - signal
     for sweep in range(ITERS):
-        whole_rows = lax.all_gather(residual, "fas", axis=1, tiled=True)
+        n_all = lax.psum(1, axis_name="fas")
+        rr = 0
+        grid = [residual]
+        while rr < n_all - 1:
+            grid.append(
+                lax.ppermute(
+                    grid[-1], axis_name="fas", perm=[(d, (d + 1) % n_all) for d in range(n_all)]
+                )
+            )
+            rr += 1
+        k_now = jnp.concatenate(grid[::-1], axis=1)
+        whole_rows = jnp.roll(k_now, (lax.axis_index("fas") + 1) * residual.shape[1], axis=1)
         gradient = lax.psum(backward_partial(whole_rows.reshape(vox_rows, BV, DIRS)), "vox")
         projected = jnp.where((weights > 0) | (gradient < 0), gradient, 0.0)
         image_pred = collect(forward_partial(projected))

time: 2240 us -> 2650 us (1.18)
  waiting for transfers between devices: 1060 us -> 1580 us
  blocking collectives: 625 us -> 507 us
    ppermute x0 -> x75, waiting for transfers between devices: none -> 530 us  [local(): lax.ppermute(grid[-1], axis_name='fas', perm=[(d, (d + 1) % n_all) for d...]
    all_gather x5 -> x0, blocking collectives: 118 us -> none  [local(): whole_rows = lax.all_gather(residual, 'fas', axis=1, tiled=True)]
  transfers between devices with their start and end apart: 16 -> 91, of which waited for: 16 -> 91; matrix products, arithmetic and copies ran while one was open for 0% -> 0% of each run, Pallas kernels for 0% -> 0%
where the time goes in v1:
time: 2650 us; the launch traced here: 2640 us
  waiting for transfers between devices  1580 us (60%)
  blocking collectives  507 us (19%)
  matrix products  276 us (10%)
  local copies, waits for them, and re-layouts  209 us (8%)
  other arithmetic  32.1 us (1%)
    reduce_scatter x11, waiting for transfers between devices, collect(): lax.psum_scatter(partial_value, 'fas', scatter_dimension=1, tiled=True)  773 us
    ppermute x75, waiting for transfers between devices, local(): lax.ppermute(grid[-1], axis_name='fas', perm=[(d, (d + 1) % n_all) for d...  530 us
    psum x5, blocking collectives, local(): image_sq = lax.psum(image_local, ('vox', 'fas'))  314 us
    psum x5, waiting for transfers between devices, local(): lax.psum(backward_partial(whole_rows.reshape(vox_rows, BV, DIRS)), 'vox')  278 us
    psum x5, blocking collectives, local(): grad_sq = lax.psum(jnp.sum(projected * projected), 'fas')  194 us
    dot_general x11, matrix products, forward_accumulate(): jnp.einsum('kvj,kjd->kvd', scaled, atom_blk.astype(jnp.float32), precisio...  124 us
    dot_general x11, local copies, waits for them, and re-layouts, forward_accumulate(): jnp.einsum('kvj,kjd->kvd', scaled, atom_blk.astype(jnp.float32), precisio...  94 us
    dot_general x11, matrix products, forward_accumulate(): jnp.dot(selector.T, image_blk.reshape(group_size, row_width), precision=l...  81.8 us
  transfers between devices with their start and end apart: 91, of which 91 were waited for; matrix products, arithmetic and copies ran while one was open for 0% of the time, Pallas kernels for 0%

profile of v1, /device:TPU:0, one launch (start us, length us, event | category | flops | bytes accessed | tf_op | source)
XLA Modules:
  0.0 2639.5 jit_solution(10455175167376392683)
XLA Ops:
  20.8 57.8 %gather_fusion = bf16[16384,96]{1,0:T(8,128)(2,1)} fusion(bf16[360,96]{1,0:T(8,128)(2,1)S(1)} %copy.28, s32[16384]{0:T(1024)S(1)} %broadcast_clamp_fusion), kind=kCustom, calls=%fused_computation | custom fusion | bytes 6356992 | tf_op jit(solution)/shard_map/gather | solution.py:30
  107.4 74.3 %reduce-scatter.12.cloned.1.call-done = f32[16,384]{1,0:T(8,128)} async-done(((f32[16,6144]{1,0:T(8,128)}), f32[16,384]{1,0:T(8,128)}) %reduce-scatter.12.cloned.1.call-update) | async-done | bytes 24592 | tf_op jit(solution)/shard_map/reduce_scatter | solution.py:99
  311.3 55.6 %all-reduce.6.cloned.1.call-done = f32[32768]{0:T(1024)} async-done(((f32[32768]{0:T(1024)}), f32[32768]{0:T(1024)}) %all-reduce.6.cloned.1.call-update) | async-done | bytes 131088 | tf_op jit(solution)/shard_map/psum | solution.py:116
  398.3 70.8 %reduce-scatter.14.cloned.1.call-done = f32[16,384]{1,0:T(8,128)} async-done(((f32[16,6144]{1,0:T(8,128)}), f32[16,384]{1,0:T(8,128)}) %reduce-scatter.14.cloned.1.call-update) | async-done | bytes 24592 | tf_op jit(solution)/shard_map/reduce_scatter | solution.py:99
  470.4 38.8 %psum.106 = f32[]{:T(128)} all-reduce(f32[]{:T(128)} %get-tuple-element.2461), channel_id=1, replica_groups=mesh['vox'=8,'fas'=16] {'fas'}, use_global_device_ids=true, to_apply=%region_8.10 | all-reduce | flops 1 | bytes 8 | tf_op jit(solution)/shard_map/psum | solution.py:120
  509.2 62.7 %psum.107 = f32[]{:T(128)} all-reduce(f32[]{:T(128)} %multiply_reduce_fusion.9), channel_id=1, replica_groups=mesh['vox'=8,'fas'=16] {'vox','fas'}, use_global_device_ids=true, to_apply=%region_13.15 | all-reduce | flops 1 | bytes 8 | tf_op jit(solution)/shard_map/psum | solution.py:121
  574.0 28.1 %while.211 = (s32[]{:T(128)}, f32[16,6144]{1,0:T(8,128)S(1)}, s32[]{:T(128)}, s32[256]{0:T(256)S(1)}, s32[]{:T(128)}, /*index=5*/bf16[256,64,64]{2,1,0:T(8,128)(...) while((s32[]{:T(128)}, f32[16,6144]{1,0:T(8,128)S(1)}, ...), condition=%wide.region_15.17_spmd.clone, body=%wide.region_14.16_spmd.clone.sunk | while | flops 1512153856 | bytes 31263864 | solution.py:68
  603.0 69.0 %reduce-scatter.16.cloned.1.call-done = f32[16,384]{1,0:T(8,128)} async-done(((f32[16,6144]{1,0:T(8,128)}), f32[16,384]{1,0:T(8,128)}) %reduce-scatter.16.cloned.1.call-update) | async-done | bytes 24592 | tf_op jit(solution)/shard_map/reduce_scatter | solution.py:99
  801.2 55.6 %all-reduce.8.cloned.1.call-done = f32[32768]{0:T(1024)} async-done(((f32[32768]{0:T(1024)}), f32[32768]{0:T(1024)}) %all-reduce.8.cloned.1.call-update) | async-done | bytes 131088 | tf_op jit(solution)/shard_map/psum | solution.py:116
  888.1 70.8 %reduce-scatter.18.cloned.1.call-done = f32[16,384]{1,0:T(8,128)} async-done(((f32[16,6144]{1,0:T(8,128)}), f32[16,384]{1,0:T(8,128)}) %reduce-scatter.18.cloned.1.call-update) | async-done | bytes 24592 | tf_op jit(solution)/shard_map/reduce_scatter | solution.py:99
  960.3 38.8 %psum.109 = f32[]{:T(128)} all-reduce(f32[]{:T(128)} %get-tuple-element.2459), channel_id=1, replica_groups=mesh['vox'=8,'fas'=16] {'fas'}, use_global_device_ids=true, to_apply=%region_22.24 | all-reduce | flops 1 | bytes 8 | tf_op jit(solution)/shard_map/psum | solution.py:120
  999.0 62.7 %psum.110 = f32[]{:T(128)} all-reduce(f32[]{:T(128)} %multiply_reduce_fusion.8), channel_id=1, replica_groups=mesh['vox'=8,'fas'=16] {'vox','fas'}, use_global_device_ids=true, to_apply=%region_27.29 | all-reduce | flops 1 | bytes 8 | tf_op jit(solution)/shard_map/psum | solution.py:121
  1063.9 28.2 %while.214 = (s32[]{:T(128)}, f32[16,6144]{1,0:T(8,128)S(1)}, s32[]{:T(128)}, s32[256]{0:T(256)S(1)}, s32[]{:T(128)}, /*index=5*/bf16[256,64,64]{2,1,0:T(8,128)(...) while((s32[]{:T(128)}, f32[16,6144]{1,0:T(8,128)S(1)}, ...), condition=%wide.region_29.31_spmd.clone, body=%wide.region_28.30_spmd.clone.sunk | while | flops 1512153856 | bytes 31263864 | solution.py:68
  1092.8 69.0 %reduce-scatter.20.cloned.1.call-done = f32[16,384]{1,0:T(8,128)} async-done(((f32[16,6144]{1,0:T(8,128)}), f32[16,384]{1,0:T(8,128)}) %reduce-scatter.20.cloned.1.call-update) | async-done | bytes 24592 | tf_op jit(solution)/shard_map/reduce_scatter | solution.py:99
  1291.0 55.6 %all-reduce.10.cloned.1.call-done = f32[32768]{0:T(1024)} async-done(((f32[32768]{0:T(1024)}), f32[32768]{0:T(1024)}) %all-reduce.10.cloned.1.call-update) | async-done | bytes 131088 | tf_op jit(solution)/shard_map/psum | solution.py:116
  1377.9 70.8 %reduce-scatter.22.cloned.1.call-done = f32[16,384]{1,0:T(8,128)} async-done(((f32[16,6144]{1,0:T(8,128)}), f32[16,384]{1,0:T(8,128)}) %reduce-scatter.22.cloned.1.call-update) | async-done | bytes 24592 | tf_op jit(solution)/shard_map/reduce_scatter | solution.py:99
  1450.1 38.7 %psum.112 = f32[]{:T(128)} all-reduce(f32[]{:T(128)} %get-tuple-element.2457), channel_id=1, replica_groups=mesh['vox'=8,'fas'=16] {'fas'}, use_global_device_ids=true, to_apply=%region_36.38 | all-reduce | flops 1 | bytes 8 | tf_op jit(solution)/shard_map/psum | solution.py:120
  1488.8 62.7 %psum.113 = f32[]{:T(128)} all-reduce(f32[]{:T(128)} %multiply_reduce_fusion.7), channel_id=1, replica_groups=mesh['vox'=8,'fas'=16] {'vox','fas'}, use_global_device_ids=true, to_apply=%region_41.43 | all-reduce | flops 1 | bytes 8 | tf_op jit(solution)/shard_map/psum | solution.py:121
  1553.6 28.1 %while.217 = (s32[]{:T(128)}, f32[16,6144]{1,0:T(8,128)S(1)}, s32[]{:T(128)}, s32[256]{0:T(256)S(1)}, s32[]{:T(128)}, /*index=5*/bf16[256,64,64]{2,1,0:T(8,128)(...) while((s32[]{:T(128)}, f32[16,6144]{1,0:T(8,128)S(1)}, ...), condition=%wide.region_43.45_spmd.clone, body=%wide.region_42.44_spmd.clone.sunk | while | flops 1512153856 | bytes 31263864 | solution.py:68
  1582.6 69.0 %reduce-scatter.24.cloned.1.call-done = f32[16,384]{1,0:T(8,128)} async-done(((f32[16,6144]{1,0:T(8,128)}), f32[16,384]{1,0:T(8,128)}) %reduce-scatter.24.cloned.1.call-update) | async-done | bytes 24592 | tf_op jit(solution)/shard_map/reduce_scatter | solution.py:99
  1780.8 55.6 %all-reduce.12.cloned.1.call-done = f32[32768]{0:T(1024)} async-done(((f32[32768]{0:T(1024)}), f32[32768]{0:T(1024)}) %all-reduce.12.cloned.1.call-update) | async-done | bytes 131088 | tf_op jit(solution)/shard_map/psum | solution.py:116
  1867.8 70.8 %reduce-scatter.26.cloned.1.call-done = f32[16,384]{1,0:T(8,128)} async-done(((f32[16,6144]{1,0:T(8,128)}), f32[16,384]{1,0:T(8,128)}) %reduce-scatter.26.cloned.1.call-update) | async-done | bytes 24592 | tf_op jit(solution)/shard_map/reduce_scatter | solution.py:99
  1939.9 38.8 %psum.115 = f32[]{:T(128)} all-reduce(f32[]{:T(128)} %get-tuple-element.2455), channel_id=1, replica_groups=mesh['vox'=8,'fas'=16] {'fas'}, use_global_device_ids=true, to_apply=%region_50.52 | all-reduce | flops 1 | bytes 8 | tf_op jit(solution)/shard_map/psum | solution.py:120
  1978.7 62.7 %psum.116 = f32[]{:T(128)} all-reduce(f32[]{:T(128)} %multiply_reduce_fusion.6), channel_id=1, replica_groups=mesh['vox'=8,'fas'=16] {'vox','fas'}, use_global_device_ids=true, to_apply=%region_55.57 | all-reduce | flops 1 | bytes 8 | tf_op jit(solution)/shard_map/psum | solution.py:121
  2043.5 28.1 %while.220 = (s32[]{:T(128)}, f32[16,6144]{1,0:T(8,128)S(1)}, s32[]{:T(128)}, s32[256]{0:T(256)S(1)}, s32[]{:T(128)}, /*index=5*/bf16[256,64,64]{2,1,0:T(8,128)(...) while((s32[]{:T(128)}, f32[16,6144]{1,0:T(8,128)S(1)}, ...), condition=%wide.region_57.59_spmd.clone, body=%wide.region_56.58_spmd.clone.sunk | while | flops 1512153856 | bytes 31263864 | solution.py:68
  2072.5 69.0 %reduce-scatter.28.cloned.1.call-done = f32[16,384]{1,0:T(8,128)} async-done(((f32[16,6144]{1,0:T(8,128)}), f32[16,384]{1,0:T(8,128)}) %reduce-scatter.28.cloned.1.call-update) | async-done | bytes 24592 | tf_op jit(solution)/shard_map/reduce_scatter | solution.py:99
  2270.6 55.6 %all-reduce.14.cloned.1.call-done = f32[32768]{0:T(1024)} async-done(((f32[32768]{0:T(1024)}), f32[32768]{0:T(1024)}) %all-reduce.14.cloned.1.call-update) | async-done | bytes 131088 | tf_op jit(solution)/shard_map/psum | solution.py:116
  2357.6 70.8 %reduce-scatter.30.cloned.1.call-done = f32[16,384]{1,0:T(8,128)} async-done(((f32[16,6144]{1,0:T(8,128)}), f32[16,384]{1,0:T(8,128)}) %reduce-scatter.30.cloned.1.call-update) | async-done | bytes 24592 | tf_op jit(solution)/shard_map/reduce_scatter | solution.py:99
  2429.7 38.8 %psum.118 = f32[]{:T(128)} all-reduce(f32[]{:T(128)} %get-tuple-element.2453), channel_id=1, replica_groups=mesh['vox'=8,'fas'=16] {'fas'}, use_global_device_ids=true, to_apply=%region_64.66 | all-reduce | flops 1 | bytes 8 | tf_op jit(solution)/shard_map/psum | solution.py:120
  2468.5 62.7 %psum.119 = f32[]{:T(128)} all-reduce(f32[]{:T(128)} %multiply_reduce_fusion.5), channel_id=1, replica_groups=mesh['vox'=8,'fas'=16] {'vox','fas'}, use_global_device_ids=true, to_apply=%region_69.71 | all-reduce | flops 1 | bytes 8 | tf_op jit(solution)/shard_map/psum | solution.py:121
  2533.3 28.2 %while.223 = (s32[]{:T(128)}, f32[16,6144]{1,0:T(8,128)S(1)}, s32[]{:T(128)}, s32[256]{0:T(256)S(1)}, s32[]{:T(128)}, /*index=5*/bf16[256,64,64]{2,1,0:T(8,128)(...) while((s32[]{:T(128)}, f32[16,6144]{1,0:T(8,128)S(1)}, ...), condition=%wide.region_71.73_spmd.clone, body=%wide.region_70.72_spmd.clone.sunk | while | flops 1512153856 | bytes 31263864 | solution.py:68
  2562.3 69.1 %reduce-scatter.32.cloned.1.call-done = f32[16,384]{1,0:T(8,128)} async-done(((f32[16,6144]{1,0:T(8,128)}), f32[16,384]{1,0:T(8,128)}) %reduce-scatter.32.cloned.1.call-update) | async-done | bytes 24592 | tf_op jit(solution)/shard_map/reduce_scatter | solution.py:99
  (458 shorter events, 1172.9 us)
Async XLA Ops:
  7.2 174.5 %reduce-scatter.12.cloned.1.call-start = ((), (), s32[]{:S(2)}) async-start(), calls=%async_computation.11 | async-start | bytes 417792 | tf_op jit(solution)/shard_map/reduce_scatter | solution.py:99
  107.4 259.5 %all-reduce.6.cloned.1.call-start = ((), (), s32[]{:S(2)}) async-start(), calls=%async_computation.12 | async-start | bytes 262144 | tf_op jit(solution)/shard_map/psum | solution.py:116
  189.6 7.1 collective-permute-start.1
  203.9 7.5 collective-permute-start.3
  261.4 7.1 collective-permute-start.11
  282.8 7.7 collective-permute-start.14
  311.2 157.9 %reduce-scatter.14.cloned.1.call-start = ((), (), s32[]{:S(2)}) async-start(), calls=%async_computation.13 | async-start | bytes 417792 | tf_op jit(solution)/shard_map/reduce_scatter | solution.py:99
  398.2 273.8 %reduce-scatter.16.cloned.1.call-start = ((), (), s32[]{:S(2)}) async-start(), calls=%async_computation.14 | async-start | bytes 417792 | tf_op jit(solution)/shard_map/reduce_scatter | solution.py:99
  603.0 253.8 %all-reduce.8.cloned.1.call-start = ((), (), s32[]{:S(2)}) async-start(), calls=%async_computation.15 | async-start | bytes 262144 | tf_op jit(solution)/shard_map/psum | solution.py:116
  694.2 7.2 collective-permute-start.18
  715.7 7.1 collective-permute-start.21
  744.3 7.5 collective-permute-start.25
  751.9 7.1 collective-permute-start.26
  801.1 157.8 %reduce-scatter.18.cloned.1.call-start = ((), (), s32[]{:S(2)}) async-start(), calls=%async_computation.16 | async-start | bytes 417792 | tf_op jit(solution)/shard_map/reduce_scatter | solution.py:99
  888.1 273.8 %reduce-scatter.20.cloned.1.call-start = ((), (), s32[]{:S(2)}) async-start(), calls=%async_computation.17 | async-start | bytes 417792 | tf_op jit(solution)/shard_map/reduce_scatter | solution.py:99
  1092.8 253.8 %all-reduce.10.cloned.1.call-start = ((), (), s32[]{:S(2)}) async-start(), calls=%async_computation.18 | async-start | bytes 262144 | tf_op jit(solution)/shard_map/psum | solution.py:116
  1169.8 7.1 collective-permute-start.31
  1184.1 7.2 collective-permute-start.33
  1191.2 7.1 collective-permute-start.34
  1234.1 7.5 collective-permute-start.40
  1290.9 157.8 %reduce-scatter.22.cloned.1.call-start = ((), (), s32[]{:S(2)}) async-start(), calls=%async_computation.19 | async-start | bytes 417792 | tf_op jit(solution)/shard_map/reduce_scatter | solution.py:99
  1377.9 273.8 %reduce-scatter.24.cloned.1.call-start = ((), (), s32[]{:S(2)}) async-start(), calls=%async_computation.20 | async-start | bytes 417792 | tf_op jit(solution)/shard_map/reduce_scatter | solution.py:99
  1582.6 253.8 %all-reduce.12.cloned.1.call-start = ((), (), s32[]{:S(2)}) async-start(), calls=%async_computation.21 | async-start | bytes 262144 | tf_op jit(solution)/shard_map/psum | solution.py:116
  1673.8 7.2 collective-permute-start.48
  1723.9 7.5 collective-permute-start.55
  1780.7 157.8 %reduce-scatter.26.cloned.1.call-start = ((), (), s32[]{:S(2)}) async-start(), calls=%async_computation.22 | async-start | bytes 417792 | tf_op jit(solution)/shard_map/reduce_scatter | solution.py:99
  1867.7 273.8 %reduce-scatter.28.cloned.1.call-start = ((), (), s32[]{:S(2)}) async-start(), calls=%async_computation.23 | async-start | bytes 417792 | tf_op jit(solution)/shard_map/reduce_scatter | solution.py:99
  2072.4 253.8 %all-reduce.14.cloned.1.call-start = ((), (), s32[]{:S(2)}) async-start(), calls=%async_computation.24 | async-start | bytes 262144 | tf_op jit(solution)/shard_map/psum | solution.py:116
  2163.7 7.2 collective-permute-start.63
  2213.7 7.5 collective-permute-start.70
  2270.6 157.8 %reduce-scatter.30.cloned.1.call-start = ((), (), s32[]{:S(2)}) async-start(), calls=%async_computation.25 | async-start | bytes 417792 | tf_op jit(solution)/shard_map/reduce_scatter | solution.py:99
  2357.6 273.8 %reduce-scatter.32.cloned.1.call-start = ((), (), s32[]{:S(2)}) async-start(), calls=%async_computation.26 | async-start | bytes 417792 | tf_op jit(solution)/shard_map/reduce_scatter | solution.py:99
  (75 other events, 630.6 us)
Sparse Core Ops, SparseCore 0:
  107.5 74.1 reduce-scatter.11
  311.3 55.5 all-reduce.5
  398.3 70.6 reduce-scatter.13
  603.1 68.9 reduce-scatter.15
  801.3 55.4 all-reduce.7
  888.2 70.6 reduce-scatter.17
  1092.9 68.9 reduce-scatter.19
  1291.0 55.4 all-reduce.9
  1378.0 70.6 reduce-scatter.21
  1582.7 68.9 reduce-scatter.23
  1780.9 55.4 all-reduce.11
  1867.8 70.6 reduce-scatter.25
  2072.6 68.9 reduce-scatter.27
  2270.7 55.5 all-reduce.13
  2357.7 70.6 reduce-scatter.29
  2562.4 68.9 reduce-scatter.31
